TPU v7x, 256 devices: a whole 4x4x8 slice. The times are simulated.
256 devices in a mesh: cal: 64 (over z, y, core), gr: 4 (over x).
Axes of the slice: x: 4, y: 4, z: 8, core: 2. Of those that a mesh axis runs over, the one named last changes fastest.
Arguments:
- features: bfloat16 [131072, 4096], P('cal', 'gr'), may hold values from -6 to 6
- coef: bfloat16 [4096], P('gr'), may hold values from -0.09375 to 0.09375
- log_exposure: float32 [131072], P('cal'), may hold values from -0.7 to 0.7
- claims: float32 [131072], P('cal'), may hold values from 0 to 4
- cluster_id: int32 [131072], P('cal'), may hold values from 0 to 1023
- period: int32 [131072], P('cal'), may hold values from 0 to 127, as said below
- period_effect: float32 [128], replicated, may hold values from -0.5 to 0.5
Outputs:
- meat: float32 [4096, 4096], P('cal', 'gr')
Inputs may be any that keep to these rules, and one draw needn't show every extreme that they name: `period`: rows of index d of cal lie in periods d * 2 to (d + 1) * 2 - 1.
All inputs are finite; a program needn't handle non-finite values.
Results may differ from a plain program's by a relative error of at most 0.0044.
Values sent between devices are 32-bit elements; how exact they have to be, the bound alone decides.
A program may use at most 64 MiB of HBM per device.

v0:
```python
import jax
import jax.numpy as jnp
from jax import lax
from jax.sharding import PartitionSpec as P

CL_DEV = 16


def per_device(features, coef, log_exposure, claims, cluster_id, period, period_effect):
    rows_here = features.shape[0]
    width = features.shape[1]
    n_cal = lax.axis_size("cal")
    clusters = CL_DEV * n_cal
    local_lin = jnp.dot(features, coef, preferred_element_type=jnp.float32)
    linear = lax.psum(local_lin, "gr")
    periods = period_effect.shape[0]
    table = jnp.where(
        period[:, None] == jnp.arange(periods, dtype=jnp.int32)[None, :],
        period_effect[None, :],
        jnp.float32(0.0),
    )
    shift = jnp.sum(table, axis=1)
    resid = (claims - jnp.exp(linear + log_exposure + shift)).astype(jnp.bfloat16)
    block = min(512, rows_here)
    count = rows_here // block
    feats = features.reshape(count, block, width)
    res_b = resid.reshape(count, block)
    ids_b = cluster_id.reshape(count, block)
    cluster_range = jnp.arange(clusters, dtype=jnp.int32)

    def step(carry, item):
        feat_blk, res_blk, id_blk = item
        picks = jnp.where(
            id_blk[:, None] == cluster_range[None, :], res_blk[:, None], jnp.bfloat16(0.0)
        )
        term = lax.dot_general(
            picks, feat_blk, (((0,), (0,)), ((), ())), preferred_element_type=jnp.float32
        )
        return (carry + term, None)

    partial_scores, _ = lax.scan(
        step, jnp.zeros((clusters, width), jnp.float32), (feats, res_b, ids_b)
    )
    owned = lax.psum_scatter(partial_scores, "cal", scatter_dimension=0, tiled=True)
    full_scores = lax.all_gather(owned, "gr", axis=1, tiled=True)
    scale = jnp.float32(1.0) / jnp.float32(rows_here * n_cal)
    meat_block = lax.psum_scatter(
        lax.dot_general(
            full_scores,
            owned,
            (((0,), (0,)), ((), ())),
            precision=lax.Precision.HIGHEST,
            preferred_element_type=jnp.float32,
        ),
        "cal",
        scatter_dimension=0,
        tiled=True,
    )
    return meat_block * scale


def solution(mesh):
    placed = (P("cal", "gr"), P("gr"), P("cal"), P("cal"), P("cal"), P("cal"), P())
    return jax.shard_map(
        per_device, mesh=mesh, in_specs=placed, out_specs=P("cal", "gr"), check_vma=False
    )
```

profile of v0, /device:TPU:2, one launch (start us, length us, event | category | flops | bytes accessed | tf_op | source)
XLA Modules:
  0.0 415.5 jit_solution(18031180852784625165)
XLA Ops:
  6.5 0.0 copy-start
  6.5 0.0 copy-start.4
  6.5 0.0 copy-start.1
  6.5 0.0 copy-start.2
  6.5 0.0 copy-start.3
  6.5 0.0 reduce-scatter.3.cloned.1.call-start
  6.6 0.7 reshape.19
  7.3 3.4 fusion.11
  10.7 10.1 %psum.7 = f32[2048]{0:T(1024)S(1)} all-reduce(f32[2048]{0:T(1024)S(1)} %bitcast.16), channel_id=1, replica_groups=mesh['cal'=64,'gr'=4] {'gr'}, use_global_device_ids=true, to_apply=%region_0.0 | all-reduce | flops 2048 | bytes 16384 | tf_op jit(solution)/shard_map/psum | solution.py:15
  20.7 0.0 copy-done
  20.8 0.0 copy-done.4
  20.8 0.0 copy-done.1
  20.8 0.6 select_reduce_fusion
  21.4 0.0 copy-done.2
  21.4 0.0 copy-done.3
  21.5 22.3 %while.11 = (s32[]{:T(128)}, f32[1024,1024]{1,0:T(8,128)}, s32[4,512]{1,0:T(4,128)S(1)}, bf16[4,512]{1,0:T(4,128)(2,1)S(1)}, bf16[4,512,1024]{2,1,0:T(8,128)(2,1)}, /*index=5*/s32[]{:T(128)}, s32[]{:T(128)}) while((s32[]{:T(128)}, f32[1024,1024]{1,0:T(8,128)}, s32[4,512]{1,0:T(4,128)S(1)}, bf16[4,512]{1,0:T(4,128)(2,1)S(1)}, ...), condition=%wide.region_3.4_spmd.clone, body=%wide.region_2.3_spmd.clone.sunk | while | flops 1076887552 | bytes 9446507 | solution.py:41
  21.5 4.6 %select_add_fusion.2 = f32[1024,1024]{1,0:T(8,128)} fusion(f32[1024,1024]{1,0:T(8,128)} %get-tuple-element.107, pred[]{:T(512)S(6)} %compare.3, bf16[4,512,1024]{2,1,0:T(8,128)(2,1)} %get-tuple-element.117, s32[]{:T(128)S(6)} %copy.10, s32[512]{0:T(512)S(1)} %bitcast.15, bf16[512]{0:T(512)(128)(2,1)S(1)} %dynamic-slice_reduce_fusion.2), kind=kOutput, calls=%fused_computation.1.clone.1 | convolution fusion | flops 1076887552 | bytes 9440261 | tf_op jit(solution)/shard_map/while/body/eval_jaxpr/dot_general | solution.py:36
  26.1 5.9 %select_add_fusion.2 = f32[1024,1024]{1,0:T(8,128)} fusion(f32[1024,1024]{1,0:T(8,128)} %get-tuple-element.107, pred[]{:T(512)S(6)} %compare.3, bf16[4,512,1024]{2,1,0:T(8,128)(2,1)} %get-tuple-element.117, s32[]{:T(128)S(6)} %copy.10, s32[512]{0:T(512)S(1)} %bitcast.15, bf16[512]{0:T(512)(128)(2,1)S(1)} %dynamic-slice_reduce_fusion.2), kind=kOutput, calls=%fused_computation.1.clone.1 | convolution fusion | flops 1076887552 | bytes 9440261 | tf_op jit(solution)/shard_map/while/body/eval_jaxpr/dot_general | solution.py:36
  32.0 5.9 %select_add_fusion.2 = f32[1024,1024]{1,0:T(8,128)} fusion(f32[1024,1024]{1,0:T(8,128)} %get-tuple-element.107, pred[]{:T(512)S(6)} %compare.3, bf16[4,512,1024]{2,1,0:T(8,128)(2,1)} %get-tuple-element.117, s32[]{:T(128)S(6)} %copy.10, s32[512]{0:T(512)S(1)} %bitcast.15, bf16[512]{0:T(512)(128)(2,1)S(1)} %dynamic-slice_reduce_fusion.2), kind=kOutput, calls=%fused_computation.1.clone.1 | convolution fusion | flops 1076887552 | bytes 9440261 | tf_op jit(solution)/shard_map/while/body/eval_jaxpr/dot_general | solution.py:36
  37.9 5.9 %select_add_fusion.2 = f32[1024,1024]{1,0:T(8,128)} fusion(f32[1024,1024]{1,0:T(8,128)} %get-tuple-element.107, pred[]{:T(512)S(6)} %compare.3, bf16[4,512,1024]{2,1,0:T(8,128)(2,1)} %get-tuple-element.117, s32[]{:T(128)S(6)} %copy.10, s32[512]{0:T(512)S(1)} %bitcast.15, bf16[512]{0:T(512)(128)(2,1)S(1)} %dynamic-slice_reduce_fusion.2), kind=kOutput, calls=%fused_computation.1.clone.1 | convolution fusion | flops 1076887552 | bytes 9440261 | tf_op jit(solution)/shard_map/while/body/eval_jaxpr/dot_general | solution.py:36
  43.8 0.0 reduce-scatter.3.cloned.1.call-update
  43.8 0.0 reduce-scatter.5.cloned.1.call-start
  43.9 145.9 %reduce-scatter.3.cloned.1.call-done = f32[16,1024]{1,0:T(8,128)} async-done(((f32[1024,1024]{1,0:T(8,128)}), f32[16,1024]{1,0:T(8,128)}) %reduce-scatter.3.cloned.1.call-update) | async-done | bytes 65552 | tf_op jit(solution)/shard_map/reduce_scatter | solution.py:44
  189.7 12.6 %all_gather.3 = f32[16,4096]{1,0:T(8,128)S(1)} all-gather(f32[16,1024]{1,0:T(8,128)} %reduce-scatter.3.cloned.1.call-done), channel_id=1, replica_groups=mesh['cal'=64,'gr'=4] {'gr'}, dimensions={1}, use_global_device_ids=true | all-gather | bytes 327680 | tf_op jit(solution)/shard_map/all_gather | solution.py:45
  202.3 16.7 %fusion.12 = f32[4096,1024]{1,0:T(8,128)} fusion(f32[16,4096]{1,0:T(8,128)S(1)} %all_gather.3, f32[16,1024]{1,0:T(8,128)} %reduce-scatter.3.cloned.1.call-done), kind=kOutput, calls=%fused_computation.18 | convolution fusion | flops 805306368 | bytes 17104896 | tf_op jit(solution)/shard_map/dot_general | solution.py:48
  219.0 0.0 reduce-scatter.5.cloned.1.call-update
  219.0 187.9 %reduce-scatter.5.cloned.1.call-done = f32[64,1024]{1,0:T(8,128)} async-done(((f32[4096,1024]{1,0:T(8,128)}), f32[64,1024]{1,0:T(8,128)}) %reduce-scatter.5.cloned.1.call-update) | async-done | bytes 262160 | tf_op jit(solution)/shard_map/reduce_scatter | solution.py:47
  407.0 1.7 broadcast_multiply_fusion
  (12 shorter events, 0.2 us)
Async XLA Ops:
  6.5 14.2 %copy-start = (s32[2048]{0:T(1024)S(1)}, s32[2048]{0:T(1024)}, u32[]{:S(2)}) copy-start(s32[2048]{0:T(1024)} %param.13) | copy-start | bytes 24580
  6.5 14.2 %copy-start.4 = (f32[128]{0:T(128)S(1)}, f32[128]{0:T(128)}, u32[]{:S(2)}) copy-start(f32[128]{0:T(128)} %param.15) | copy-start | bytes 1540
  6.5 14.2 %copy-start.1 = (s32[2048]{0:T(1024)S(1)}, s32[2048]{0:T(1024)}, u32[]{:S(2)}) copy-start(s32[2048]{0:T(1024)} %param.14) | copy-start | bytes 24580
  6.5 14.9 %copy-start.2 = (f32[2048]{0:T(1024)S(1)}, f32[2048]{0:T(1024)}, u32[]{:S(2)}) copy-start(f32[2048]{0:T(1024)} %param.12) | copy-start | bytes 24580
  6.5 14.9 %copy-start.3 = (f32[2048]{0:T(1024)S(1)}, f32[2048]{0:T(1024)}, u32[]{:S(2)}) copy-start(f32[2048]{0:T(1024)} %param.11) | copy-start | bytes 24580
  6.5 183.2 %reduce-scatter.3.cloned.1.call-start = ((), (), s32[]{:S(2)}) async-start(), calls=%async_computation.2 | async-start | bytes 4259840 | tf_op jit(solution)/shard_map/reduce_scatter | solution.py:44
  43.8 363.2 %reduce-scatter.5.cloned.1.call-start = ((), (), s32[]{:S(2)}) async-start(), calls=%async_computation.3 | async-start | bytes 17039360 | tf_op jit(solution)/shard_map/reduce_scatter | solution.py:47
Sparse Core Ops, SparseCore 0:
  43.9 145.7 reduce-scatter.2
  219.1 187.7 reduce-scatter.4
where the time goes:
time: 416 us; the launch traced here: 415 us
  waiting for transfers between devices  334 us (80%)
  matrix products  42.2 us (10%)
  blocking collectives  22.6 us (5%)
  between operations  13.5 us (3%)
    reduce_scatter x1, waiting for transfers between devices, per_device(): lax.psum_scatter(lax.dot_general(full_scores, owned, (((0,), (0,)), ((),...  188 us
    reduce_scatter x1, waiting for transfers between devices, per_device(): lax.psum_scatter(partial_scores, 'cal', scatter_dimension=0, tiled=True)  146 us
    dot_general x4, matrix products, step(): lax.dot_general(picks, feat_blk, (((0,), (0,)), ((), ())), preferred_elem...  22.2 us
    dot_general x1, matrix products, per_device(): lax.dot_general(full_scores, owned, (((0,), (0,)), ((), ())), precision=l...  16.7 us
    all_gather x1, blocking collectives, per_device(): full_scores = lax.all_gather(owned, 'gr', axis=1, tiled=True)  12.6 us
    psum x1, blocking collectives, per_device(): linear = lax.psum(local_lin, 'gr')  10.1 us
  transfers between devices with their start and end apart: 2, of which 2 were waited for; matrix products, arithmetic and copies ran while one was open for 0% of the time, Pallas kernels for 0%

commit v1 on v0

--- a/solution.py
+++ b/solution.py
@@ -42,7 +42,16 @@
         step, jnp.zeros((clusters, width), jnp.float32), (feats, res_b, ids_b)
     )
     owned = lax.psum_scatter(partial_scores, "cal", scatter_dimension=0, tiled=True)
-    full_scores = lax.all_gather(owned, "gr", axis=1, tiled=True)
+    ways = lax.axis_size("gr")
+    up = [(d, (d + 1) % ways) for d in range(ways)]
+    down = [(d, (d - 1) % ways) for d in range(ways)]
+    earlier, later = ([owned], [owned])
+    for _ in range(ways // 2):
+        earlier.append(lax.ppermute(earlier[-1], "gr", up))
+    for _ in range((ways - 1) // 2):
+        later.append(lax.ppermute(later[-1], "gr", down))
+    line = jnp.concatenate([*earlier[::-1], *later[1:]], axis=1)
+    full_scores = jnp.roll(line, (lax.axis_index("gr") - ways // 2) * owned.shape[1], axis=1)
     scale = jnp.float32(1.0) / jnp.float32(rows_here * n_cal)
     meat_block = lax.psum_scatter(
         lax.dot_general(

time: 416 us -> 416 us (level)
  blocking collectives: 22.6 us -> 10.1 us
  waiting for transfers between devices: 334 us -> 341 us
    all_gather x1 -> x0, blocking collectives: 12.6 us -> none  [per_device(): full_scores = lax.all_gather(owned, 'gr', axis=1, tiled=True)]
    ppermute x0 -> x3, waiting for transfers between devices: none -> 6.06 us  [the longest x2 5.25 us: per_device(): earlier.append(lax.ppermute(earlier[-1], 'gr', up))]
  transfers between devices with their start and end apart: 2 -> 5, of which waited for: 2 -> 5; matrix products, arithmetic and copies ran while one was open for 0% -> 0% of each run, Pallas kernels for 0% -> 0%
where the time goes in v1:
time: 416 us
  waiting for transfers between devices  341 us (82%)
  matrix products  42.3 us (10%)
  between operations  13.5 us (3%)
  blocking collectives  10.1 us (2%)
    reduce_scatter x1, waiting for transfers between devices, per_device(): lax.psum_scatter(lax.dot_general(full_scores, owned, (((0,), (0,)), ((),...  189 us
    reduce_scatter x1, waiting for transfers between devices, per_device(): lax.psum_scatter(partial_scores, 'cal', scatter_dimension=0, tiled=True)  146 us
    dot_general x4, matrix products, step(): lax.dot_general(picks, feat_blk, (((0,), (0,)), ((), ())), preferred_elem...  22.2 us
    dot_general x1, matrix products, per_device(): lax.dot_general(full_scores, owned, (((0,), (0,)), ((), ())), precision=l...  16.7 us
    psum x1, blocking collectives, per_device(): linear = lax.psum(local_lin, 'gr')  10.1 us
  transfers between devices with their start and end apart: 5, of which 5 were waited for; matrix products, arithmetic and copies ran while one was open for 0% of the time, Pallas kernels for 0%

profile of v1, /device:TPU:2, one launch (start us, length us, event | category | flops | bytes accessed | tf_op | source)
XLA Modules:
  0.0 415.7 jit_solution(13559465136922048671)
XLA Ops:
  6.5 0.0 copy-start
  6.5 0.0 copy-start.4
  6.5 0.0 reduce-scatter.3.cloned.1.call-start
  6.6 0.7 reshape.19
  7.3 3.4 fusion.14
  10.7 10.1 %psum.7 = f32[2048]{0:T(1024)S(1)} all-reduce(f32[2048]{0:T(1024)S(1)} %bitcast.15), channel_id=1, replica_groups=mesh['cal'=64,'gr'=4] {'gr'}, use_global_device_ids=true, to_apply=%region_0.0 | all-reduce | flops 2048 | bytes 16384 | tf_op jit(solution)/shard_map/psum | solution.py:15
  20.7 0.0 copy-done
  20.8 0.0 copy-done.4
  20.8 0.0 copy-done.1
  20.8 0.6 select_reduce_fusion
  21.4 0.0 copy-done.2
  21.4 0.0 copy-done.3
  21.5 22.4 %while.11 = (s32[]{:T(128)}, f32[1024,1024]{1,0:T(8,128)}, s32[4,512]{1,0:T(4,128)S(1)}, bf16[4,512]{1,0:T(4,128)(2,1)S(1)}, bf16[4,512,1024]{2,1,0:T(8,128)(2,1)}, /*index=5*/s32[]{:T(128)}, s32[]{:T(128)}) while((s32[]{:T(128)}, f32[1024,1024]{1,0:T(8,128)}, s32[4,512]{1,0:T(4,128)S(1)}, bf16[4,512]{1,0:T(4,128)(2,1)S(1)}, ...), condition=%wide.region_3.4_spmd.clone, body=%wide.region_2.3_spmd.clone.sunk | while | flops 1076887552 | bytes 9446507 | solution.py:41
  21.5 4.6 %select_add_fusion.2 = f32[1024,1024]{1,0:T(8,128)} fusion(f32[1024,1024]{1,0:T(8,128)} %get-tuple-element.107, pred[]{:T(512)S(6)} %compare.4, bf16[4,512,1024]{2,1,0:T(8,128)(2,1)} %get-tuple-element.117, s32[]{:T(128)S(6)} %copy.10, s32[512]{0:T(512)S(1)} %bitcast.14, bf16[512]{0:T(512)(128)(2,1)S(1)} %dynamic-slice_reduce_fusion.2), kind=kOutput, calls=%fused_computation.1.clone.1 | convolution fusion | flops 1076887552 | bytes 9440261 | tf_op jit(solution)/shard_map/while/body/eval_jaxpr/dot_general | solution.py:36
  26.1 5.9 %select_add_fusion.2 = f32[1024,1024]{1,0:T(8,128)} fusion(f32[1024,1024]{1,0:T(8,128)} %get-tuple-element.107, pred[]{:T(512)S(6)} %compare.4, bf16[4,512,1024]{2,1,0:T(8,128)(2,1)} %get-tuple-element.117, s32[]{:T(128)S(6)} %copy.10, s32[512]{0:T(512)S(1)} %bitcast.14, bf16[512]{0:T(512)(128)(2,1)S(1)} %dynamic-slice_reduce_fusion.2), kind=kOutput, calls=%fused_computation.1.clone.1 | convolution fusion | flops 1076887552 | bytes 9440261 | tf_op jit(solution)/shard_map/while/body/eval_jaxpr/dot_general | solution.py:36
  32.0 5.9 %select_add_fusion.2 = f32[1024,1024]{1,0:T(8,128)} fusion(f32[1024,1024]{1,0:T(8,128)} %get-tuple-element.107, pred[]{:T(512)S(6)} %compare.4, bf16[4,512,1024]{2,1,0:T(8,128)(2,1)} %get-tuple-element.117, s32[]{:T(128)S(6)} %copy.10, s32[512]{0:T(512)S(1)} %bitcast.14, bf16[512]{0:T(512)(128)(2,1)S(1)} %dynamic-slice_reduce_fusion.2), kind=kOutput, calls=%fused_computation.1.clone.1 | convolution fusion | flops 1076887552 | bytes 9440261 | tf_op jit(solution)/shard_map/while/body/eval_jaxpr/dot_general | solution.py:36
  38.0 5.9 %select_add_fusion.2 = f32[1024,1024]{1,0:T(8,128)} fusion(f32[1024,1024]{1,0:T(8,128)} %get-tuple-element.107, pred[]{:T(512)S(6)} %compare.4, bf16[4,512,1024]{2,1,0:T(8,128)(2,1)} %get-tuple-element.117, s32[]{:T(128)S(6)} %copy.10, s32[512]{0:T(512)S(1)} %bitcast.14, bf16[512]{0:T(512)(128)(2,1)S(1)} %dynamic-slice_reduce_fusion.2), kind=kOutput, calls=%fused_computation.1.clone.1 | convolution fusion | flops 1076887552 | bytes 9440261 | tf_op jit(solution)/shard_map/while/body/eval_jaxpr/dot_general | solution.py:36
  43.8 0.0 reduce-scatter.3.cloned.1.call-update
  43.9 0.0 reduce-scatter.5.cloned.1.call-start
  43.9 145.9 %reduce-scatter.3.cloned.1.call-done = f32[16,1024]{1,0:T(8,128)} async-done(((f32[1024,1024]{1,0:T(8,128)}), f32[16,1024]{1,0:T(8,128)}) %reduce-scatter.3.cloned.1.call-update) | async-done | bytes 65552 | tf_op jit(solution)/shard_map/reduce_scatter | solution.py:44
  189.8 1.5 collective-permute-start
  191.3 3.0 collective-permute-done
  194.3 1.5 collective-permute-start.1
  195.8 0.6 collective-permute-start.2
  196.3 2.2 collective-permute-done.1
  198.6 0.8 constant_dynamic-update-slice_fusion.5
  199.5 0.8 collective-permute-done.2
  200.3 0.8 constant_dynamic-update-slice_fusion.1
  201.1 16.7 %fusion.11 = f32[4096,1024]{1,0:T(8,128)} fusion(f32[16,1024]{1,0:T(8,128)} %reduce-scatter.3.cloned.1.call-done, f32[16,8192]{1,0:T(8,128)S(1)} %constant_dynamic-update-slice_fusion, s32[]{:T(128)S(6)} %select_n.23), kind=kOutput, calls=%fused_computation.15 | convolution fusion | flops 805306368 | bytes 17104900 | tf_op jit(solution)/shard_map/dot_general | solution.py:57
  217.8 0.0 reduce-scatter.5.cloned.1.call-update
  217.8 189.4 %reduce-scatter.5.cloned.1.call-done = f32[64,1024]{1,0:T(8,128)} async-done(((f32[4096,1024]{1,0:T(8,128)}), f32[64,1024]{1,0:T(8,128)}) %reduce-scatter.5.cloned.1.call-update) | async-done | bytes 262160 | tf_op jit(solution)/shard_map/reduce_scatter | solution.py:56
  407.2 1.7 broadcast_multiply_fusion
  (21 shorter events, 0.2 us)
Async XLA Ops:
  6.5 14.2 %copy-start = (s32[2048]{0:T(1024)S(1)}, s32[2048]{0:T(1024)}, u32[]{:S(2)}) copy-start(s32[2048]{0:T(1024)} %param.13) | copy-start | bytes 24580
  6.5 14.2 %copy-start.4 = (f32[128]{0:T(128)S(1)}, f32[128]{0:T(128)}, u32[]{:S(2)}) copy-start(f32[128]{0:T(128)} %param.15) | copy-start | bytes 1540
  6.5 14.2 %copy-start.1 = (s32[2048]{0:T(1024)S(1)}, s32[2048]{0:T(1024)}, u32[]{:S(2)}) copy-start(s32[2048]{0:T(1024)} %param.14) | copy-start | bytes 24580
  6.5 14.9 %copy-start.2 = (f32[2048]{0:T(1024)S(1)}, f32[2048]{0:T(1024)}, u32[]{:S(2)}) copy-start(f32[2048]{0:T(1024)} %param.12) | copy-start | bytes 24580
  6.5 14.9 %copy-start.3 = (f32[2048]{0:T(1024)S(1)}, f32[2048]{0:T(1024)}, u32[]{:S(2)}) copy-start(f32[2048]{0:T(1024)} %param.11) | copy-start | bytes 24580
  6.5 183.3 %reduce-scatter.3.cloned.1.call-start = ((), (), s32[]{:S(2)}) async-start(), calls=%async_computation.2 | async-start | bytes 4259840 | tf_op jit(solution)/shard_map/reduce_scatter | solution.py:44
  43.9 363.4 %reduce-scatter.5.cloned.1.call-start = ((), (), s32[]{:S(2)}) async-start(), calls=%async_computation.3 | async-start | bytes 17039360 | tf_op jit(solution)/shard_map/reduce_scatter | solution.py:56
  189.8 4.5 %collective-permute-start = (f32[16,1024]{1,0:T(8,128)}, f32[16,1024]{1,0:T(8,128)S(1)}, u32[]{:S(2)}, u32[]{:S(2)}) collective-permute-start(f32[16,1024]{1,0:T(8,128)} %reduce-scatter.3.cloned.1.call-done), channel_id=1, source_target_pairs={{0,1},{1,2},{2,3},{3,0},{4,5},{5,6},{6,7},{7,4},{8,9},{9,10},{10,1... | collective-permute-start | bytes 196616 | tf_op jit(solution)/shard_map/ppermute | solution.py:50
  194.3 4.3 %collective-permute-start.1 = (f32[16,1024]{1,0:T(8,128)S(1)}, f32[16,1024]{1,0:T(8,128)S(1)}, u32[]{:S(2)}, u32[]{:S(2)}) collective-permute-start(f32[16,1024]{1,0:T(8,128)S(1)} %collective-permute-done), channel_id=1, source_target_pairs={{0,1},{1,2},{2,3},{3,0},{4,5},{5,6},{6,7},{7,4},{8,9},{9,10},{10,1... | collective-permute-start | bytes 196616 | tf_op jit(solution)/shard_map/ppermute | solution.py:50
  195.8 4.5 %collective-permute-start.2 = (f32[16,1024]{1,0:T(8,128)}, f32[16,1024]{1,0:T(8,128)S(1)}, u32[]{:S(2)}, u32[]{:S(2)}) collective-permute-start(f32[16,1024]{1,0:T(8,128)} %reduce-scatter.3.cloned.1.call-done), channel_id=1, source_target_pairs={{0,3},{1,0},{2,1},{3,2},{4,7},{5,4},{6,5},{7,6},{8,11},{9,8},{10,9... | collective-permute-start | bytes 196616 | tf_op jit(solution)/shard_map/ppermute | solution.py:52
Sparse Core Ops, SparseCore 0:
  44.0 145.8 reduce-scatter.2
  218.0 189.2 reduce-scatter.4
